TPU v7x, 128 devices: a whole 4x4x4 slice. The times are simulated.
128 devices in a mesh: bank: 4 (over y_hi, core), gal: 32 (over z, y_lo, x).
Axes of the slice: x: 4, y: 4 (y_hi: 2, y_lo: 2; y = y_hi * 2 + y_lo), z: 4, core: 2. Of those that a mesh axis runs over, the one named last changes fastest.
Arguments:
- querybank: bfloat16 [16384, 512], P(('bank', 'gal')), may hold values from -80 to 80
- gallery: bfloat16 [131072, 512], P('gal'), may hold values from -80 to 80
- test_queries: bfloat16 [2048, 512], P(('bank', 'gal')), may hold values from -80 to 80
Outputs:
- retrieval: float32 [2048, 32, 4096], P(None, 'gal', 'bank')
All inputs are finite; a program needn't handle non-finite values.
Results may differ from a plain program's by a relative error of at most 0.0017.
Values may be sent and summed in bfloat16 or wider, within the bound.
A program may use at most 64 MiB of HBM per device.

v0:
```python
import jax
import jax.numpy as jnp
from jax import lax
from jax.sharding import PartitionSpec as P

inverse_temp = 20.0
epsilon = 1e-06


def unit_rows(values):
    wide = values.astype(jnp.float32)
    return (wide * lax.rsqrt(jnp.sum(wide * wide, axis=-1, keepdims=True) + epsilon)).astype(
        jnp.bfloat16
    )


def exp_sums(piece, clips_t):
    rows = piece.shape[0]
    blocks = piece.reshape(rows // 512, 512, piece.shape[1])

    def one_block(total, block):
        sims = jnp.dot(block, clips_t, preferred_element_type=jnp.float32)
        return (total + jnp.sum(jnp.exp(inverse_temp * sims), axis=0), None)

    start_total = jnp.zeros((clips_t.shape[1],), jnp.float32)
    total, unused = lax.scan(one_block, start_total, blocks)
    return total


def local(querybank, gallery, test_queries):
    clips_t = unit_rows(gallery).T
    captions = unit_rows(querybank)
    tests = unit_rows(test_queries)
    groups = lax.axis_size("bank")
    count = captions.shape[0] * lax.axis_size("gal") * groups
    share = clips_t.shape[1] // groups
    partial_sums = exp_sums(lax.all_gather(captions, "gal", axis=0, tiled=True), clips_t)
    totals = lax.psum(partial_sums, "bank")
    mine = lax.dynamic_slice_in_dim(totals, lax.axis_index("bank") * share, share, 0)
    every_test = lax.all_gather(tests, ("bank", "gal"), axis=0, tiled=True)
    columns = lax.dynamic_slice_in_dim(clips_t, lax.axis_index("bank") * share, share, 1)
    sims = jnp.dot(every_test, columns, preferred_element_type=jnp.float32)
    result = inverse_temp * sims - jnp.log(mine / count)[None, :]
    return result[:, None, :]


def solution(mesh):
    placed = (P(("bank", "gal"), None), P("gal", None), P(("bank", "gal"), None))
    return jax.shard_map(
        local, mesh=mesh, in_specs=placed, out_specs=P(None, "gal", "bank"), check_vma=False
    )
```

profile of v0, /device:TPU:1, one launch (start us, length us, event | category | flops | bytes accessed | tf_op | source)
XLA Modules:
  0.0 500.7 jit_solution(5182620168477035748)
XLA Ops:
  6.5 1.0 fusion.6
  7.6 1.6 fusion.7
  9.2 0.0 all-gather.3.cloned.1.call-start
  9.3 0.8 fusion.8
  10.1 1.4 fusion.9
  11.6 6.3 %copy.4 = bf16[4096,512]{0,1:T(8,128)(2,1)} copy(bf16[4096,512]{1,0:T(8,128)(2,1)} %param.6) | data formatting | bytes 8388608 | tf_op args[1]
  17.9 3.2 fusion.3
  21.1 0.2 copy-done
  21.3 2.9 fusion.13
  24.2 2.8 fusion.4
  27.0 122.1 %all-gather.5.cloned.1.call-done = bf16[4096,512]{1,0:T(8,128)(2,1)} async-done(((bf16[128,512]{1,0:T(8,128)(2,1)}), bf16[4096,512]{1,0:T(8,128)(2,1)}) %all-gather.5.cloned.1.call-update) | async-done | bytes 4194320 | tf_op jit(solution)/shard_map/all_gather | solution.py:37
  149.1 38.5 %while.11 = (s32[]{:T(128)}, f32[4096]{0:T(1024)S(1)}, bf16[8,512,512]{2,1,0:T(8,128)(2,1)}, bf16[512,4096]{1,0:T(8,128)(2,1)}, s32[]{:T(128)}, /*index=5*/s32[]{:T(128)}) while((s32[]{:T(128)}, f32[4096]{0:T(1024)S(1)}, bf16[8,512,512]{2,1,0:T(8,128)(2,1)}, bf16[512,4096]{1,0:T(8,128)(2,1)}, s32[]{:T(128)}, ...), condition=%wide.region_5.6_spmd.clone, body=%wide.region_3.5_spmd.clone.sunk | while | flops 2151682048 | bytes 4784219 | solution.py:26
  149.1 4.8 exponential_reduce_fusion.2
  153.9 4.8 exponential_reduce_fusion.2
  158.7 4.8 exponential_reduce_fusion.2
  163.5 4.8 exponential_reduce_fusion.2
  168.4 4.8 exponential_reduce_fusion.2
  173.2 4.8 exponential_reduce_fusion.2
  178.0 4.8 exponential_reduce_fusion.2
  182.8 4.8 exponential_reduce_fusion.2
  187.6 32.3 %psum.7 = f32[4096]{0:T(1024)S(1)} all-reduce(f32[4096]{0:T(1024)S(1)} %get-tuple-element.27), channel_id=1, replica_groups=mesh['bank'=4,'gal'=32] {'bank'}, use_global_device_ids=true, to_apply=%region_6.7 | all-reduce | flops 4096 | bytes 32768 | tf_op jit(solution)/shard_map/psum | solution.py:38
  219.9 253.6 %all-gather.3.cloned.1.call-done = bf16[2048,512]{1,0:T(8,128)(2,1)} async-done(((bf16[16,512]{1,0:T(8,128)(2,1)}), bf16[2048,512]{1,0:T(8,128)(2,1)}) %all-gather.3.cloned.1.call-update) | async-done | bytes 2097168 | tf_op jit(solution)/shard_map/all_gather | solution.py:40
  473.5 4.2 subtract_bitcast_fusion
  477.8 16.1 %copy.5 = f32[2048,1,1024]{2,1,0:T(1,128)} copy(f32[2048,1,1024]{2,0,1:T(8,128)S(1)} %subtract_bitcast_fusion) | data formatting | bytes 16777216 | tf_op jit(solution)/shard_map/broadcast_in_dim | solution.py:44
  (17 shorter events, 0.1 us)
Async XLA Ops:
  6.5 142.6 %all-gather.5.cloned.1.call-start = ((), (), s32[]{:S(2)}) async-start(), calls=%async_computation.1 | async-start | bytes 4325376 | tf_op jit(solution)/shard_map/all_gather | solution.py:37
  9.2 464.3 %all-gather.3.cloned.1.call-start = ((), (), s32[]{:S(2)}) async-start(), calls=%async_computation | async-start | bytes 2113536 | tf_op jit(solution)/shard_map/all_gather | solution.py:40
  17.9 3.4 copy-start
Sparse Core Ops, SparseCore 0:
  9.4 139.7 all-gather.4
  150.8 322.6 all-gather.2
where the time goes:
time: 501 us
  waiting for transfers between devices  376 us (75%)
  matrix products  42.4 us (8%)
  blocking collectives  32.3 us (6%)
  local copies, waits for them, and re-layouts  22.7 us (5%)
  other arithmetic  13.9 us (3%)
  between operations  13.5 us (3%)
    all_gather x1, waiting for transfers between devices, local(): every_test = lax.all_gather(tests, ('bank', 'gal'), axis=0, tiled=True)  254 us
    all_gather x1, waiting for transfers between devices, local(): lax.all_gather(captions, 'gal', axis=0, tiled=True)  122 us
    dot_general x8, matrix products, one_block(): sims = jnp.dot(block, clips_t, preferred_element_type=jnp.float32)  38.2 us
    psum x1, blocking collectives, local(): totals = lax.psum(partial_sums, 'bank')  32.3 us
    broadcast_in_dim x1, local copies, waits for them, and re-layouts, local(): return result[:, None, :]  16.1 us
  transfers between devices with their start and end apart: 2, of which 2 were waited for; matrix products, arithmetic and copies ran while one was open for 11% of the time, Pallas kernels for 0%

commit v1 on v0

--- a/solution.py
+++ b/solution.py
@@ -37,7 +37,10 @@
     partial_sums = exp_sums(lax.all_gather(captions, "gal", axis=0, tiled=True), clips_t)
     totals = lax.psum(partial_sums, "bank")
     mine = lax.dynamic_slice_in_dim(totals, lax.axis_index("bank") * share, share, 0)
-    every_test = lax.all_gather(tests, ("bank", "gal"), axis=0, tiled=True)
+    every_test = jnp.concatenate(
+        lax.all_to_all(jnp.stack([tests] * lax.axis_size(("bank", "gal"))), ("bank", "gal"), 0, 0),
+        axis=0,
+    )
     columns = lax.dynamic_slice_in_dim(clips_t, lax.axis_index("bank") * share, share, 1)
     sims = jnp.dot(every_test, columns, preferred_element_type=jnp.float32)
     result = inverse_temp * sims - jnp.log(mine / count)[None, :]

time: 501 us -> 256 us (0.51)
  waiting for transfers between devices: 376 us -> 119 us
  starting transfers between devices: 0.04 us -> 11.5 us
    all_gather x1 -> x0, waiting for transfers between devices: 254 us -> none  [local(): every_test = lax.all_gather(tests, ('bank', 'gal'), axis=0, tiled=True)]
    all_to_all x0 -> x1, starting transfers between devices: none -> 11.5 us  [local(): lax.all_to_all(jnp.stack([tests] * lax.axis_size(('bank', 'gal'))), ('ban...]
  transfers between devices with their start and end apart: 2 -> 2, of which waited for: 2 -> 1; matrix products, arithmetic and copies ran while one was open for 11% -> 22% of each run, Pallas kernels for 0% -> 0%
where the time goes in v1:
time: 256 us
  waiting for transfers between devices  119 us (46%)
  matrix products  41.8 us (16%)
  blocking collectives  32.3 us (13%)
  local copies, waits for them, and re-layouts  24.4 us (10%)
  between operations  13.5 us (5%)
  other arithmetic  13.3 us (5%)
  starting transfers between devices  11.5 us (4%)
    all_gather x1, waiting for transfers between devices, local(): lax.all_gather(captions, 'gal', axis=0, tiled=True)  119 us
    dot_general x8, matrix products, one_block(): sims = jnp.dot(block, clips_t, preferred_element_type=jnp.float32)  38.2 us
    psum x1, blocking collectives, local(): totals = lax.psum(partial_sums, 'bank')  32.3 us
    broadcast_in_dim x1, local copies, waits for them, and re-layouts, local(): return result[:, None, :]  16.1 us
    all_to_all x1, starting transfers between devices, local(): lax.all_to_all(jnp.stack([tests] * lax.axis_size(('bank', 'gal'))), ('ban...  11.5 us
    unnamed x3, local copies, waits for them, and re-layouts  6.58 us
    convert_element_type x3, other arithmetic, unit_rows(): (wide * lax.rsqrt(jnp.sum(wide * wide, axis=-1, keepdims=True) + epsilon)...  5.24 us
  transfers between devices with their start and end apart: 2, of which 1 were waited for; matrix products, arithmetic and copies ran while one was open for 22% of the time, Pallas kernels for 0%

profile of v1, /device:TPU:1, one launch (start us, length us, event | category | flops | bytes accessed | tf_op | source)
XLA Modules:
  0.0 255.7 jit_solution(3991031435777105618)
XLA Ops:
  6.5 1.0 fusion.6
  7.6 1.6 fusion.7
  9.2 0.8 fusion.8
  10.1 0.8 fusion.9
  10.9 1.7 stack.2
  12.5 11.5 %all-to-all-start = ((bf16[128,16,512]{2,1,0:T(8,128)(2,1)}), bf16[128,16,512]{2,1,0:T(8,128)(2,1)S(1)}, u32[]{:S(2)}, u32[]{:S(2)}) async-start(bf16[128,16,512]{2,1,0:T(8,128)(2,1)} %stack.2), calls=%async_computation | async-start | bytes 4194304 | tf_op jit(solution)/shard_map/all_to_all | solution.py:41
  24.0 6.3 %copy.4 = bf16[4096,512]{0,1:T(8,128)(2,1)} copy(bf16[4096,512]{1,0:T(8,128)(2,1)} %param.6) | data formatting | bytes 8388608 | tf_op args[1]
  30.4 3.2 %fusion.3 = f32[4096]{0:T(1024)S(1)} fusion(bf16[4096,512]{0,1:T(8,128)(2,1)} %copy.4), kind=kLoop, calls=%fused_computation.7 | loop fusion | flops 6287360 | bytes 4210688 | tf_op jit(solution)/shard_map/reduce_sum | solution.py:12
  33.6 0.2 copy-done
  33.9 2.9 %fusion.13 = bf16[512,4096]{1,0:T(8,128)(2,1)} fusion(f32[4096]{0:T(1024)S(1)} %add_rsqrt_fusion, bf16[4096,512]{0,1:T(8,128)(2,1)S(1)} %copy-done), kind=kLoop, calls=%fused_computation.24 | loop fusion | flops 6291456 | bytes 8404992 | tf_op jit(solution)/shard_map/transpose | solution.py:31
  36.8 2.8 %fusion.4 = bf16[4096,512]{0,1:T(8,128)(2,1)} fusion(bf16[4096,512]{0,1:T(8,128)(2,1)S(1)} %copy-done, f32[4096]{0:T(1024)S(1)} %add_rsqrt_fusion), kind=kLoop, calls=%fused_computation.8 | loop fusion | flops 6291456 | bytes 8404992 | tf_op jit(solution)/shard_map/convert_element_type | solution.py:12
  39.6 118.7 %all-gather.2.cloned.1.call-done = bf16[4096,512]{1,0:T(8,128)(2,1)} async-done(((bf16[128,512]{1,0:T(8,128)(2,1)}), bf16[4096,512]{1,0:T(8,128)(2,1)}) %all-gather.2.cloned.1.call-update) | async-done | bytes 4194320 | tf_op jit(solution)/shard_map/all_gather | solution.py:37
  158.3 38.5 %while.11 = (s32[]{:T(128)}, f32[4096]{0:T(1024)S(1)}, bf16[8,512,512]{2,1,0:T(8,128)(2,1)}, bf16[512,4096]{1,0:T(8,128)(2,1)}, s32[]{:T(128)}, /*index=5*/s32[]{:T(128)}) while((s32[]{:T(128)}, f32[4096]{0:T(1024)S(1)}, bf16[8,512,512]{2,1,0:T(8,128)(2,1)}, bf16[512,4096]{1,0:T(8,128)(2,1)}, s32[]{:T(128)}, ...), condition=%wide.region_5.6_spmd.clone, body=%wide.region_3.5_spmd.clone.sunk | while | flops 2151682048 | bytes 4784219 | solution.py:26
  158.3 4.8 %exponential_reduce_fusion.2 = f32[4096]{0:T(1024)S(1)} fusion(bf16[512,4096]{1,0:T(8,128)(2,1)} %get-tuple-element.91, bf16[8,512,512]{2,1,0:T(8,128)(2,1)} %get-tuple-element.90, s32[]{:T(128)S(6)} %copy.8), kind=kOutput, calls=%fused_computation.clone.1 | convolution fusion | flops 2151673856 | bytes 4734980 | tf_op jit(solution)/shard_map/while/body/eval_jaxpr/dot_general | solution.py:22
  163.1 4.8 %exponential_reduce_fusion.2 = f32[4096]{0:T(1024)S(1)} fusion(bf16[512,4096]{1,0:T(8,128)(2,1)} %get-tuple-element.91, bf16[8,512,512]{2,1,0:T(8,128)(2,1)} %get-tuple-element.90, s32[]{:T(128)S(6)} %copy.8), kind=kOutput, calls=%fused_computation.clone.1 | convolution fusion | flops 2151673856 | bytes 4734980 | tf_op jit(solution)/shard_map/while/body/eval_jaxpr/dot_general | solution.py:22
  167.9 4.8 %exponential_reduce_fusion.2 = f32[4096]{0:T(1024)S(1)} fusion(bf16[512,4096]{1,0:T(8,128)(2,1)} %get-tuple-element.91, bf16[8,512,512]{2,1,0:T(8,128)(2,1)} %get-tuple-element.90, s32[]{:T(128)S(6)} %copy.8), kind=kOutput, calls=%fused_computation.clone.1 | convolution fusion | flops 2151673856 | bytes 4734980 | tf_op jit(solution)/shard_map/while/body/eval_jaxpr/dot_general | solution.py:22
  172.7 4.8 %exponential_reduce_fusion.2 = f32[4096]{0:T(1024)S(1)} fusion(bf16[512,4096]{1,0:T(8,128)(2,1)} %get-tuple-element.91, bf16[8,512,512]{2,1,0:T(8,128)(2,1)} %get-tuple-element.90, s32[]{:T(128)S(6)} %copy.8), kind=kOutput, calls=%fused_computation.clone.1 | convolution fusion | flops 2151673856 | bytes 4734980 | tf_op jit(solution)/shard_map/while/body/eval_jaxpr/dot_general | solution.py:22
  177.5 4.8 %exponential_reduce_fusion.2 = f32[4096]{0:T(1024)S(1)} fusion(bf16[512,4096]{1,0:T(8,128)(2,1)} %get-tuple-element.91, bf16[8,512,512]{2,1,0:T(8,128)(2,1)} %get-tuple-element.90, s32[]{:T(128)S(6)} %copy.8), kind=kOutput, calls=%fused_computation.clone.1 | convolution fusion | flops 2151673856 | bytes 4734980 | tf_op jit(solution)/shard_map/while/body/eval_jaxpr/dot_general | solution.py:22
  182.3 4.8 %exponential_reduce_fusion.2 = f32[4096]{0:T(1024)S(1)} fusion(bf16[512,4096]{1,0:T(8,128)(2,1)} %get-tuple-element.91, bf16[8,512,512]{2,1,0:T(8,128)(2,1)} %get-tuple-element.90, s32[]{:T(128)S(6)} %copy.8), kind=kOutput, calls=%fused_computation.clone.1 | convolution fusion | flops 2151673856 | bytes 4734980 | tf_op jit(solution)/shard_map/while/body/eval_jaxpr/dot_general | solution.py:22
  187.1 4.8 %exponential_reduce_fusion.2 = f32[4096]{0:T(1024)S(1)} fusion(bf16[512,4096]{1,0:T(8,128)(2,1)} %get-tuple-element.91, bf16[8,512,512]{2,1,0:T(8,128)(2,1)} %get-tuple-element.90, s32[]{:T(128)S(6)} %copy.8), kind=kOutput, calls=%fused_computation.clone.1 | convolution fusion | flops 2151673856 | bytes 4734980 | tf_op jit(solution)/shard_map/while/body/eval_jaxpr/dot_general | solution.py:22
  191.9 4.8 %exponential_reduce_fusion.2 = f32[4096]{0:T(1024)S(1)} fusion(bf16[512,4096]{1,0:T(8,128)(2,1)} %get-tuple-element.91, bf16[8,512,512]{2,1,0:T(8,128)(2,1)} %get-tuple-element.90, s32[]{:T(128)S(6)} %copy.8), kind=kOutput, calls=%fused_computation.clone.1 | convolution fusion | flops 2151673856 | bytes 4734980 | tf_op jit(solution)/shard_map/while/body/eval_jaxpr/dot_general | solution.py:22
  196.7 32.3 %psum.7 = f32[4096]{0:T(1024)S(1)} all-reduce(f32[4096]{0:T(1024)S(1)} %get-tuple-element.27), channel_id=1, replica_groups=mesh['bank'=4,'gal'=32] {'bank'}, use_global_device_ids=true, to_apply=%region_6.7 | all-reduce | flops 4096 | bytes 32768 | tf_op jit(solution)/shard_map/psum | solution.py:38
  229.1 3.6 %subtract_bitcast_fusion = f32[2048,1,1024]{2,0,1:T(8,128)S(1)} fusion(bf16[2048,512]{1,0:T(8,128)(2,1)S(1)} %bitcast.15, f32[1024]{0:T(1024)S(1)} %multiply_log_fusion, bf16[4096,512]{0,1:T(8,128)(2,1)} %fusion.4, s32[]{:T(128)S(6)} %select_n.4), kind=kOutput, calls=%fused_computation.9 | convolution fusion | flops 2151677952 | bytes 11538436 | tf_op jit(solution)/shard_map/dot_general | solution.py:45
  232.7 16.1 %copy.5 = f32[2048,1,1024]{2,1,0:T(1,128)} copy(f32[2048,1,1024]{2,0,1:T(8,128)S(1)} %subtract_bitcast_fusion) | data formatting | bytes 16777216 | tf_op jit(solution)/shard_map/broadcast_in_dim | solution.py:47
  (17 shorter events, 0.1 us)
Async XLA Ops:
  6.5 151.7 %all-gather.2.cloned.1.call-start = ((), (), s32[]{:S(2)}) async-start(), calls=%async_computation.1 | async-start | bytes 4325376 | tf_op jit(solution)/shard_map/all_gather | solution.py:37
  12.5 216.5 %all-to-all-start = ((bf16[128,16,512]{2,1,0:T(8,128)(2,1)}), bf16[128,16,512]{2,1,0:T(8,128)(2,1)S(1)}, u32[]{:S(2)}, u32[]{:S(2)}) async-start(bf16[128,16,512]{2,1,0:T(8,128)(2,1)} %stack.2), calls=%async_computation | async-start | bytes 4194304 | tf_op jit(solution)/shard_map/all_to_all | solution.py:41
  30.4 3.5 %copy-start = (bf16[4096,512]{0,1:T(8,128)(2,1)S(1)}, bf16[4096,512]{0,1:T(8,128)(2,1)}, u32[]{:S(2)}) copy-start(bf16[4096,512]{0,1:T(8,128)(2,1)} %copy.4) | copy-start | bytes 12582916
Sparse Core Ops, SparseCore 0:
  9.4 148.8 all-gather.1
